TPU v7x, 256 devices: a whole 4x4x8 slice. The times are simulated.
256 devices in a mesh: dp: 2 (over core), blk: 16 (over z, x_hi), head: 8 (over x_lo, y).
Axes of the slice: x: 4 (x_hi: 2, x_lo: 2; x = x_hi * 2 + x_lo), y: 4, z: 8, core: 2. Of those that a mesh axis runs over, the one named last changes fastest.
Arguments:
- queries: bfloat16 [16384, 5120], P(('dp', 'blk'), 'head'), parts along dimension 0, may hold values from -20 to 20, as said below
- keys: bfloat16 [16384, 5120], P(('dp', 'blk'), 'head'), parts along dimension 0, may hold values from -20 to 20
- values: bfloat16 [16384, 5120], P(('dp', 'blk'), 'head'), parts along dimension 0, may hold values from -6 to 6
- block_list: int32 [128, 16], P(('dp', 'blk')), parts along dimension 0, may hold values from 0 to 63, as said below
- block_count: int32 [128], P(('dp', 'blk')), parts along dimension 0, may hold values from 4 to 16, as said below
- out_weight: bfloat16 [5120, 5120], P('head'), may hold values from -0.25 to 0.25
Outputs:
- projected: bfloat16 [16384, 5120], P(('dp', 'blk', 'head')), parts along dimension 0
There are 2 independent parts, one for each index of `dp`. A program takes and returns all parts, laid end to end along the dimension named above; an argument that names none is the same for every part. Nothing has to cross between parts.
Inputs may be any that keep to these rules, and one draw needn't show every extreme that they name: `block_list`: each row names 16 different key blocks of the same clip; its first entry is the query block itself; only the first block_count entries of a row are used. `block_count`: some query block uses all 16 entries in every draw. `queries`: query entries lie in the stated range.
All inputs are finite; a program needn't handle non-finite values.
Results may differ from a plain program's by a relative error of at most 0.02.
Values may be sent and summed in bfloat16 or wider, within the bound.
No kernel may reach another device: no remote copies, remote signals or barrier semaphores. Data moves between devices by JAX's collectives and lax.ppermute only.
A program may use at most 128 MiB of HBM per device.

v0:
```python
import math
import jax
import jax.numpy as jnp
from jax import lax
from jax.sharding import PartitionSpec as P

HD = 128
BS = 128
KB = 16


def on_device(queries, keys, values, block_list, block_count, out_weight):
    tok_rows, feature_width = queries.shape
    head_count = feature_width // HD
    query_blocks = tok_rows // BS
    block_total = tok_rows * lax.axis_size("blk") // BS
    score_scale = 1.0 / math.sqrt(HD)
    query_heads = queries.reshape(tok_rows, head_count, HD)
    block_range = jnp.arange(block_total, dtype=jnp.int32)
    listed = jnp.arange(KB, dtype=jnp.int32)[None, :] < block_count[:, None]
    matches = listed[:, :, None] & (block_list[:, :, None] == block_range[None, None, :])
    allowed = jnp.sum(jnp.where(matches, 1.0, 0.0), axis=1).astype(jnp.float32)

    def attend(state_in, key_piece, value_piece, row_start):
        running, totals, summed = state_in
        row_count = key_piece.shape[0]
        piece_blocks = (row_start + jnp.arange(row_count, dtype=jnp.int32)) // BS
        onehot = jnp.where(piece_blocks[:, None] == block_range[None, :], 1.0, 0.0).astype(
            jnp.float32
        )
        columns = jnp.einsum("bn,pn->bp", allowed, onehot)
        visible = jnp.broadcast_to(
            columns[:, None, :] > 0.5, (query_blocks, BS, row_count)
        ).reshape(tok_rows, row_count)
        scores = (
            jnp.einsum(
                "qhd,khd->hqk",
                query_heads,
                key_piece.reshape(row_count, head_count, HD),
                preferred_element_type=jnp.float32,
            )
            * score_scale
        )
        scores = jnp.where(visible[None], scores, -jnp.inf)
        highest = jnp.maximum(running, jnp.max(scores, axis=-1))
        weights = jnp.where(visible[None], jnp.exp(scores - highest[:, :, None]), 0.0)
        rescale = jnp.exp(running - highest)
        totals = totals * rescale + jnp.sum(weights, axis=-1)
        update = jnp.einsum(
            "hqk,khd->qhd",
            weights.astype(jnp.bfloat16),
            value_piece.reshape(row_count, head_count, HD),
            preferred_element_type=jnp.float32,
        )
        summed = summed * jnp.transpose(rescale)[:, :, None] + update
        return (highest, totals, summed)

    initial = (
        jnp.full((head_count, tok_rows), -1e30, jnp.float32),
        jnp.zeros((head_count, tok_rows), jnp.float32),
        jnp.zeros((tok_rows, head_count, HD), jnp.float32),
    )
    key_piece = lax.all_gather(keys, "blk", axis=0, tiled=True)
    value_piece = lax.all_gather(values, "blk", axis=0, tiled=True)
    row_count = key_piece.shape[0]
    sub_rows = 512
    key_split = key_piece.reshape(row_count // sub_rows, sub_rows, feature_width)
    value_split = value_piece.reshape(row_count // sub_rows, sub_rows, feature_width)
    offsets = sub_rows * jnp.arange(row_count // sub_rows, dtype=jnp.int32)

    def advance(inner_state, packed):
        key_sub, value_sub, offset_now = packed
        return (attend(inner_state, key_sub, value_sub, offset_now), None)

    finished, unused = lax.scan(advance, initial, (key_split, value_split, offsets))
    running, totals, summed = finished
    attended = (
        (summed / jnp.transpose(totals)[:, :, None])
        .astype(jnp.bfloat16)
        .reshape(tok_rows, feature_width)
    )
    return lax.psum_scatter(
        jnp.dot(attended, out_weight, preferred_element_type=jnp.float32).astype(jnp.bfloat16),
        "head",
        scatter_dimension=0,
        tiled=True,
    )


def solution(mesh):
    placed = (
        P(("dp", "blk"), "head"),
        P(("dp", "blk"), "head"),
        P(("dp", "blk"), "head"),
        P(("dp", "blk"), None),
        P(("dp", "blk")),
        P("head", None),
    )
    return jax.shard_map(
        on_device,
        mesh=mesh,
        in_specs=placed,
        out_specs=P(("dp", "blk", "head"), None),
        check_vma=False,
    )
```

profile of v0, /device:TPU:1, one launch (start us, length us, event | category | flops | bytes accessed | tf_op | source)
XLA Modules:
  0.0 660.4 jit_solution(10925951334080078393)
XLA Ops:
  11.3 158.9 %all-gather.3.cloned.1.call-done = bf16[8192,640]{1,0:T(8,128)(2,1)} async-done(((bf16[512,640]{1,0:T(8,128)(2,1)}), bf16[8192,640]{1,0:T(8,128)(2,1)}) %all-gather.3.cloned.1.call-update) | async-done | bytes 10485776 | tf_op jit(solution)/shard_map/all_gather | solution.py:63
  170.2 156.2 %all-gather.5.cloned.1.call-done = bf16[8192,640]{1,0:T(8,128)(2,1)} async-done(((bf16[512,640]{1,0:T(8,128)(2,1)}), bf16[8192,640]{1,0:T(8,128)(2,1)}) %all-gather.5.cloned.1.call-update) | async-done | bytes 10485776 | tf_op jit(solution)/shard_map/all_gather | solution.py:64
  326.4 254.1 %while.17 = (s32[]{:T(128)}, f32[5,512]{1,0:T(8,128)S(1)}, f32[5,512]{1,0:T(8,128)S(1)}, f32[512,5,128]{0,2,1:T(8,128)}, s32[16]{0:T(128)S(1)}, /*index=5*/bf16[...) while((s32[]{:T(128)}, f32[5,512]{1,0:T(8,128)S(1)}, ...), condition=%wide.region_4.5_spmd.clone, body=%wide.region_1.4_spmd.clone.sunk | while | flops 689464320 | bytes 43037372 | solution.py:75
  328.1 1.6 broadcast_in_dim.150
  329.8 1.4 constant_dynamic-slice_fusion.3
  331.5 3.5 fusion.55
  335.3 5.3 fusion.59
  343.6 1.6 broadcast_in_dim.150
  345.4 1.4 constant_dynamic-slice_fusion.3
  347.0 3.4 fusion.55
  350.8 5.7 fusion.59
  359.5 1.6 broadcast_in_dim.150
  361.3 1.4 constant_dynamic-slice_fusion.3
  362.9 3.4 fusion.55
  366.7 5.7 fusion.59
  375.4 1.6 broadcast_in_dim.150
  377.2 1.4 constant_dynamic-slice_fusion.3
  378.9 3.5 fusion.55
  382.6 5.7 fusion.59
  391.3 1.6 broadcast_in_dim.150
  393.1 1.4 constant_dynamic-slice_fusion.3
  394.8 3.4 fusion.55
  398.5 5.7 fusion.59
  407.3 1.6 broadcast_in_dim.150
  409.0 1.4 constant_dynamic-slice_fusion.3
  410.7 3.5 fusion.55
  414.4 5.7 fusion.59
  423.2 1.6 broadcast_in_dim.150
  424.9 1.4 constant_dynamic-slice_fusion.3
  426.6 3.4 fusion.55
  430.3 5.7 fusion.59
  439.1 1.6 broadcast_in_dim.150
  440.8 1.4 constant_dynamic-slice_fusion.3
  442.5 3.5 fusion.55
  446.2 5.7 fusion.59
  455.0 1.6 broadcast_in_dim.150
  456.7 1.4 constant_dynamic-slice_fusion.3
  458.4 3.4 fusion.55
  462.1 5.7 fusion.59
  470.9 1.6 broadcast_in_dim.150
  474.3 3.5 fusion.55
  478.0 5.7 fusion.59
  486.8 1.6 broadcast_in_dim.150
  490.2 3.4 fusion.55
  493.9 5.7 fusion.59
  502.7 1.6 broadcast_in_dim.150
  506.1 3.5 fusion.55
  509.9 5.7 fusion.59
  518.6 1.6 broadcast_in_dim.150
  522.0 3.4 fusion.55
  525.8 5.7 fusion.59
  534.5 1.6 broadcast_in_dim.150
  537.9 3.5 fusion.55
  541.7 5.7 fusion.59
  550.4 1.6 broadcast_in_dim.150
  552.2 1.4 constant_dynamic-slice_fusion.3
  553.8 3.4 fusion.55
  557.6 5.7 fusion.59
  566.3 1.6 broadcast_in_dim.150
  569.7 3.5 fusion.55
  573.5 5.7 fusion.59
  580.5 1.5 divide_convert_fusion
  582.0 8.9 %convolution_convert_fusion = bf16[512,5120]{1,0:T(8,128)(2,1)} fusion(bf16[512,640]{0,1:T(8,128)(2,1)S(1)} %bitcast.84, bf16[640,5120]{1,0:T(8,128)(2,1)} %param.13), kind=kOutput, calls=%fused_computation.40 | convolution fusion | flops 3358064640 | bytes 12451840 | tf_op jit(solution)/shard_map/dot_general | solution.py:83
  590.9 63.0 %reduce-scatter.2.cloned.1.call-done = bf16[64,5120]{1,0:T(8,128)(2,1)} async-done(((bf16[512,5120]{1,0:T(8,128)(2,1)}), bf16[64,5120]{1,0:T(8,128)(2,1)}) %reduce-scatter.2.cloned.1.call-update) | async-done | bytes 655376 | tf_op jit(solution)/shard_map/reduce_scatter | solution.py:82
  (276 shorter events, 71.1 us)
Async XLA Ops:
  6.5 163.6 %all-gather.3.cloned.1.call-start = ((), (), s32[]{:S(2)}) async-start(), calls=%async_computation.1 | async-start | bytes 11141120 | tf_op jit(solution)/shard_map/all_gather | solution.py:63
  7.3 319.2 %all-gather.5.cloned.1.call-start = ((), (), s32[]{:S(2)}) async-start(), calls=%async_computation.2 | async-start | bytes 11141120 | tf_op jit(solution)/shard_map/all_gather | solution.py:64
  8.0 645.9 %reduce-scatter.2.cloned.1.call-start = ((), (), s32[]{:S(2)}) async-start(), calls=%async_computation.3 | async-start | bytes 5898240 | tf_op jit(solution)/shard_map/reduce_scatter | solution.py:82
  335.0 5.6 slice-start
  335.2 5.4 slice-start.1
  350.5 6.0 slice-start
  350.8 5.7 slice-start.1
  366.4 6.0 slice-start
  366.7 5.7 slice-start.1
  382.3 6.0 slice-start
  382.6 5.7 slice-start.1
  398.2 6.0 slice-start
  398.5 5.7 slice-start.1
  414.1 6.0 slice-start
  414.4 5.7 slice-start.1
  430.0 6.0 slice-start
  430.3 5.7 slice-start.1
  445.9 6.0 slice-start
  446.2 5.7 slice-start.1
  461.9 6.0 slice-start
  462.1 5.7 slice-start.1
  477.8 6.0 slice-start
  478.0 5.7 slice-start.1
  493.7 6.0 slice-start
  493.9 5.7 slice-start.1
  509.6 6.0 slice-start
  509.8 5.7 slice-start.1
  525.5 6.0 slice-start
  525.7 5.7 slice-start.1
  541.4 6.0 slice-start
  541.7 5.7 slice-start.1
  557.3 6.0 slice-start
  557.6 5.7 slice-start.1
  573.2 6.0 slice-start
  573.5 5.7 slice-start.1
Sparse Core Ops, SparseCore 0:
  9.9 160.1 all-gather.2
  172.8 153.6 all-gather.4
  591.1 62.7 reduce-scatter.1
where the time goes:
time: 661 us; the launch traced here: 660 us
  waiting for transfers between devices  380 us (57%)
  matrix products  159 us (24%)
  local copies, waits for them, and re-layouts  72.9 us (11%)
  other arithmetic  33.8 us (5%)
  between operations  13.2 us (2%)
    all_gather x1, waiting for transfers between devices, on_device(): key_piece = lax.all_gather(keys, 'blk', axis=0, tiled=True)  159 us
    all_gather x1, waiting for transfers between devices, on_device(): value_piece = lax.all_gather(values, 'blk', axis=0, tiled=True)  156 us
    dot_general x16, matrix products, attend(): jnp.einsum('hqk,khd->qhd', weights.astype(jnp.bfloat16), value_piece.resh...  91.3 us
    reduce_scatter x1, waiting for transfers between devices, on_device(): lax.psum_scatter(jnp.dot(attended, out_weight, preferred_element_type=jnp...  63 us
    dot_general x16, matrix products, attend(): jnp.einsum('qhd,khd->hqk', query_heads, key_piece.reshape(row_count, head...  55.1 us
    dynamic_slice x64, local copies, waits for them, and re-layouts, on_device(): lax.scan(advance, initial, (key_split, value_split, offsets))  40.1 us
    broadcast_in_dim x16, local copies, waits for them, and re-layouts, attend(): jnp.broadcast_to(columns[:, None, :] > 0.5, (query_blocks, BS, row_count))  25.6 us
    reduce_sum x16, other arithmetic, attend(): totals = totals * rescale + jnp.sum(weights, axis=-1)  20.3 us
  transfers between devices with their start and end apart: 3, of which 3 were waited for; matrix products, arithmetic and copies ran while one was open for 0% of the time, Pallas kernels for 0%

commit v1 on v0

--- a/solution.py
+++ b/solution.py
@@ -60,7 +60,9 @@
         jnp.zeros((head_count, tok_rows), jnp.float32),
         jnp.zeros((tok_rows, head_count, HD), jnp.float32),
     )
-    key_piece = lax.all_gather(keys, "blk", axis=0, tiled=True)
+    key_piece = jnp.concatenate(
+        lax.all_to_all(jnp.stack([keys] * lax.axis_size("blk")), "blk", 0, 0), axis=0
+    )
     value_piece = lax.all_gather(values, "blk", axis=0, tiled=True)
     row_count = key_piece.shape[0]
     sub_rows = 512

time: 661 us -> 695 us (1.051)
  local copies, waits for them, and re-layouts: 72.9 us -> 88.5 us
  starting transfers between devices: 0.08 us -> 11.8 us
    all_to_all x0 -> x1, waiting for transfers between devices: none -> 274 us  [on_device(): lax.all_to_all(jnp.stack([keys] * lax.axis_size('blk')), 'blk', 0, 0)]
    all_gather x1 -> x0, waiting for transfers between devices: 159 us -> none  [on_device(): key_piece = lax.all_gather(keys, 'blk', axis=0, tiled=True)]
    all_gather x1, waiting for transfers between devices: 156 us -> 47.2 us  [on_device(): value_piece = lax.all_gather(values, 'blk', axis=0, tiled=True)]
    all_to_all x0 -> x1, starting transfers between devices: none -> 11.8 us  [on_device(): lax.all_to_all(jnp.stack([keys] * lax.axis_size('blk')), 'blk', 0, 0)]
    dynamic_slice x64, local copies, waits for them, and re-layouts: 40.1 us -> 50.5 us  [on_device(): lax.scan(advance, initial, (key_split, value_split, offsets))]
where the time goes in v1:
time: 695 us; the launch traced here: 693 us
  waiting for transfers between devices  386 us (56%)
  matrix products  160 us (23%)
  local copies, waits for them, and re-layouts  88.5 us (13%)
  other arithmetic  32.2 us (5%)
  between operations  13.5 us (2%)
  starting transfers between devices  11.8 us (2%)
    all_to_all x1, waiting for transfers between devices, on_device(): lax.all_to_all(jnp.stack([keys] * lax.axis_size('blk')), 'blk', 0, 0)  274 us
    dot_general x16, matrix products, attend(): jnp.einsum('hqk,khd->qhd', weights.astype(jnp.bfloat16), value_piece.resh...  91.4 us
    reduce_scatter x1, waiting for transfers between devices, on_device(): lax.psum_scatter(jnp.dot(attended, out_weight, preferred_element_type=jnp...  64.1 us
    dot_general x16, matrix products, attend(): jnp.einsum('qhd,khd->hqk', query_heads, key_piece.reshape(row_count, head...  55.5 us
    dynamic_slice x64, local copies, waits for them, and re-layouts, on_device(): lax.scan(advance, initial, (key_split, value_split, offsets))  50.5 us
    all_gather x1, waiting for transfers between devices, on_device(): value_piece = lax.all_gather(values, 'blk', axis=0, tiled=True)  47.2 us
    broadcast_in_dim x16, local copies, waits for them, and re-layouts, attend(): jnp.broadcast_to(columns[:, None, :] > 0.5, (query_blocks, BS, row_count))  25.6 us
    reduce_sum x16, other arithmetic, attend(): totals = totals * rescale + jnp.sum(weights, axis=-1)  20.3 us
  transfers between devices with their start and end apart: 3, of which 3 were waited for; matrix products, arithmetic and copies ran while one was open for 0% of the time, Pallas kernels for 0%

profile of v1, /device:TPU:1, one launch (start us, length us, event | category | flops | bytes accessed | tf_op | source)
XLA Modules:
  0.0 693.0 jit_solution(3315080071847672241)
XLA Ops:
  6.5 1.3 copy.19
  7.9 5.0 stack.2
  12.8 11.8 %all-to-all-start = ((bf16[16,512,640]{1,2,0:T(8,128)(2,1)}), bf16[16,512,640]{1,2,0:T(8,128)(2,1)}, u32[]{:S(2)}, u32[]{:S(2)}) async-start(bf16[16,512,640]{1,2,0:T(8,128)(2,1)} %stack.2), calls=%async_computation | async-start | bytes 20971520 | tf_op jit(solution)/shard_map/all_to_all | solution.py:64
  26.2 273.7 %all-to-all-done = bf16[16,512,640]{1,2,0:T(8,128)(2,1)} async-done(((bf16[16,512,640]{1,2,0:T(8,128)(2,1)}), bf16[16,512,640]{1,2,0:T(8,128)(2,1)}, u32[]{:S(2)}, u32[]{:S(2)}) %all-to-all-start) | async-done | bytes 10485792 | tf_op jit(solution)/shard_map/all_to_all | solution.py:64
  299.9 47.2 %all-gather.2.cloned.1.call-done = bf16[8192,640]{1,0:T(8,128)(2,1)} async-done(((bf16[512,640]{1,0:T(8,128)(2,1)}), bf16[8192,640]{1,0:T(8,128)(2,1)}) %all-gather.2.cloned.1.call-update) | async-done | bytes 10485776 | tf_op jit(solution)/shard_map/all_gather | solution.py:66
  347.1 264.6 %while.17 = (s32[]{:T(128)}, f32[5,512]{1,0:T(8,128)S(1)}, f32[5,512]{1,0:T(8,128)S(1)}, f32[512,5,128]{0,2,1:T(8,128)}, s32[16]{0:T(128)S(1)}, /*index=5*/bf16[...) while((s32[]{:T(128)}, f32[5,512]{1,0:T(8,128)S(1)}, ...), condition=%wide.region_4.5_spmd.clone, body=%wide.region_1.4_spmd.clone.sunk | while | flops 689464320 | bytes 41726656 | solution.py:77
  348.8 1.6 broadcast_in_dim.150
  351.7 3.5 fusion.55
  356.6 5.4 fusion.59
  361.9 1.3 fusion.57
  364.9 1.6 broadcast_in_dim.150
  367.8 3.5 fusion.55
  372.8 5.7 fusion.59
  378.5 1.3 fusion.57
  381.5 1.6 broadcast_in_dim.150
  384.4 3.5 fusion.55
  389.3 5.7 fusion.59
  395.1 1.3 fusion.57
  398.1 1.6 broadcast_in_dim.150
  401.0 3.5 fusion.55
  405.9 5.7 fusion.59
  411.6 1.3 fusion.57
  414.6 1.6 broadcast_in_dim.150
  417.5 3.5 fusion.55
  422.4 5.7 fusion.59
  428.2 1.3 fusion.57
  431.2 1.6 broadcast_in_dim.150
  434.1 3.5 fusion.55
  439.0 5.7 fusion.59
  444.8 1.3 fusion.57
  447.8 1.6 broadcast_in_dim.150
  450.7 3.5 fusion.55
  455.6 5.7 fusion.59
  461.3 1.3 fusion.57
  464.3 1.6 broadcast_in_dim.150
  467.2 3.5 fusion.55
  472.1 5.7 fusion.59
  480.9 1.6 broadcast_in_dim.150
  483.8 3.5 fusion.55
  488.7 5.7 fusion.59
  497.5 1.6 broadcast_in_dim.150
  500.3 3.5 fusion.55
  505.3 5.7 fusion.59
  514.0 1.6 broadcast_in_dim.150
  516.9 3.5 fusion.55
  521.8 5.7 fusion.59
  530.6 1.6 broadcast_in_dim.150
  533.5 3.5 fusion.55
  538.4 5.7 fusion.59
  547.2 1.6 broadcast_in_dim.150
  550.0 3.5 fusion.55
  555.0 5.7 fusion.59
  563.7 1.6 broadcast_in_dim.150
  566.6 3.5 fusion.55
  571.5 5.7 fusion.59
  580.3 1.6 broadcast_in_dim.150
  583.2 3.5 fusion.55
  588.1 5.7 fusion.59
  596.8 1.6 broadcast_in_dim.150
  599.7 3.5 fusion.55
  604.7 5.7 fusion.59
  611.7 1.5 divide_convert_fusion
  613.2 8.9 %convolution_convert_fusion = bf16[512,5120]{1,0:T(8,128)(2,1)} fusion(bf16[512,640]{0,1:T(8,128)(2,1)S(1)} %bitcast.82, bf16[640,5120]{1,0:T(8,128)(2,1)} %param.13), kind=kOutput, calls=%fused_computation.40 | convolution fusion | flops 3358064640 | bytes 12451840 | tf_op jit(solution)/shard_map/dot_general | solution.py:85
  622.1 64.1 %reduce-scatter.2.cloned.1.call-done = bf16[64,5120]{1,0:T(8,128)(2,1)} async-done(((bf16[512,5120]{1,0:T(8,128)(2,1)}), bf16[64,5120]{1,0:T(8,128)(2,1)}) %reduce-scatter.2.cloned.1.call-update) | async-done | bytes 655376 | tf_op jit(solution)/shard_map/reduce_scatter | solution.py:84
  (283 shorter events, 83.3 us)
Async XLA Ops:
  12.8 12.6 %copy-start = (bf16[512,640]{1,0:T(8,128)(2,1)S(1)}, bf16[512,640]{1,0:T(8,128)(2,1)}, u32[]{:S(2)}) copy-start(bf16[512,640]{1,0:T(8,128)(2,1)} %param.8) | copy-start | bytes 1966084
  12.8 13.2 %copy-start.2 = (s32[4]{0:T(128)S(1)}, s32[4]{0:T(128)}, u32[]{:S(2)}) copy-start(s32[4]{0:T(128)} %param.12) | copy-start | bytes 52
  12.8 13.3 %copy-start.1 = (s32[4,16]{1,0:T(4,128)S(1)}, s32[4,16]{1,0:T(4,128)}, u32[]{:S(2)}) copy-start(s32[4,16]{1,0:T(4,128)} %param.11) | copy-start | bytes 772
  12.8 287.0 %all-to-all-start = ((bf16[16,512,640]{1,2,0:T(8,128)(2,1)}), bf16[16,512,640]{1,2,0:T(8,128)(2,1)}, u32[]{:S(2)}, u32[]{:S(2)}) async-start(bf16[16,512,640]{1,2,0:T(8,128)(2,1)} %stack.2), calls=%async_computation | async-start | bytes 20971520 | tf_op jit(solution)/shard_map/all_to_all | solution.py:64
  24.6 322.5 %all-gather.2.cloned.1.call-start = ((), (), s32[]{:S(2)}) async-start(), calls=%async_computation.2 | async-start | bytes 11141120 | tf_op jit(solution)/shard_map/all_gather | solution.py:66
  25.3 660.8 %reduce-scatter.2.cloned.1.call-start = ((), (), s32[]{:S(2)}) async-start(), calls=%async_computation.3 | async-start | bytes 5898240 | tf_op jit(solution)/shard_map/reduce_scatter | solution.py:84
  356.3 5.6 slice-start
  356.6 5.4 slice-start.1
  372.5 6.0 slice-start
  372.7 5.8 slice-start.1
  389.0 6.0 slice-start
  389.3 5.8 slice-start.1
  405.6 6.0 slice-start
  405.9 5.8 slice-start.1
  422.2 6.0 slice-start
  422.4 5.8 slice-start.1
  438.7 6.0 slice-start
  439.0 5.8 slice-start.1
  455.3 6.0 slice-start
  455.6 5.8 slice-start.1
  471.9 6.0 slice-start
  472.1 5.8 slice-start.1
  488.4 6.0 slice-start
  488.7 5.8 slice-start.1
  505.0 6.0 slice-start
  505.3 5.8 slice-start.1
  521.5 6.0 slice-start
  521.8 5.8 slice-start.1
  538.1 6.0 slice-start
  538.4 5.8 slice-start.1
  554.7 6.0 slice-start
  554.9 5.8 slice-start.1
  571.2 6.0 slice-start
  571.5 5.8 slice-start.1
  587.8 6.0 slice-start
  588.1 5.8 slice-start.1
  604.4 6.0 slice-start
  604.6 5.8 slice-start.1
Sparse Core Ops, SparseCore 0:
  28.0 319.0 all-gather.1
  622.2 63.8 reduce-scatter.1
